TPU v7x, 512 devices: a whole 4x8x8 slice. The times are simulated.
512 devices in a mesh: blk: 128 (over z, y, core), dir: 4 (over x).
Axes of the slice: x: 4, y: 8, z: 8, core: 2. Of those that a mesh axis runs over, the one named last changes fastest.
Arguments:
- spectrum: float32 [36, 36, 2048, 128], P('dir', None, 'blk'), may hold values from 0 to 4.5, as said below
- group_speed: float32 [36, 2048, 128], P(None, 'blk'), may hold values from 0.3 to 1
- ocean_current: float32 [2, 128, 2048], P(None, 'blk'), may hold values from -0.5 to 0.5
- route_slot: int32 [2048, 128], P('blk'), may hold values from -1 to 2047, as said below
- wind_vector: float32 [128, 2, 2048], P('blk'), may hold values from -4 to 4
- ice_cover: float32 [128, 2048], P('blk'), may hold values from 0 to 0.9
Outputs:
- spectrum_out: float32 [36, 36, 2048, 128], P('dir', None, 'blk')
- ocean_forcing: float32 [4, 128, 2048], P('dir', 'blk')
Inputs may be any that keep to these rules, and one draw needn't show every extreme that they name: `route_slot`: on one geographic block the sea cells routed to one owner use slots 0 to their count - 1, at most 16 of them; some owner receives 16 cells from every block. Land cells hold -1. `spectrum`: positive everywhere.
All inputs are finite; a program needn't handle non-finite values.
Results may differ from a plain program's by a relative error of at most 0.00002.
Values sent between devices are 32-bit elements; how exact they have to be, the bound alone decides.
No kernel may reach another device: no remote copies, remote signals or barrier semaphores. Data moves between devices by JAX's collectives and lax.ppermute only.
A program may use at most 64 MiB of HBM per device.

v0:
```python
import jax
import jax.numpy as jnp
from jax import lax
from jax.sharding import Mesh
from jax.sharding import PartitionSpec as P

BLK = ("blk_0", "blk_1", "blk_2")


COURANT = 0.15
WIND_GROWTH = 0.15
DAMP_RATE = 0.5
STEEP_COEF = 0.01
STRESS_SCALE = 1.0
STOKES_SCALE = 0.15
RATIO_STEP = 1.1


def cut_along(value, dim, size):
    dims = value.shape
    pieces = value.reshape(*dims[:dim], size, dims[dim] // size, *dims[dim + 1 :])
    return jnp.moveaxis(pieces, dim, 0)


def laid_out(pieces, dim):
    pieces = jnp.moveaxis(pieces, 0, dim)
    dims = pieces.shape
    return pieces.reshape(*dims[:dim], dims[dim] * dims[dim + 1], *dims[dim + 2 :])


def turned_blocks(pieces, axes, order):
    inside = pieces.shape[1:]
    filled = pieces.reshape(*(lax.axis_size(a) for a in axes), *inside)
    for k in order:
        filled = lax.all_to_all(filled, axes[k], k, k, tiled=True)
    return filled.reshape(-1, *inside)


def two_step_exchange(value, groups, order, split_dim, concat_dim):
    size = lax.axis_size(groups[0]) * lax.axis_size(groups[1])
    pieces = cut_along(value, split_dim, size)
    return laid_out(turned_blocks(pieces, groups, order), concat_dim)


def with_halo(value, sides, width):
    for axis, dim in sides:
        size, length = (lax.axis_size(axis), value.shape[dim])
        up = [(i, (i + 1) % size) for i in range(size - 1)]
        down = [(j, i) for i, j in up]
        last = lax.slice_in_dim(value, length - width, length, axis=dim)
        initial = lax.slice_in_dim(value, 0, width, axis=dim)
        before = lax.ppermute(last, axis, up)
        after = lax.ppermute(initial, axis, down)
        value = jnp.concatenate([before, value, after], axis=dim)
    return value


def in_one_piece(arrays, axis, split_dim, concat_dim, along):
    widths = [a.shape[along] for a in arrays]
    both = jnp.concatenate(arrays, axis=along)
    filled = lax.all_to_all(both, axis, split_axis=split_dim, concat_axis=concat_dim, tiled=True)
    return tuple(jnp.split(filled, [sum(widths[:k]) for k in range(1, len(widths))], axis=along))


def summed_on_arrival(value, axis, dim):
    pieces = cut_along(value, dim, lax.axis_size(axis))
    arrived = lax.all_to_all(pieces, axis, split_axis=0, concat_axis=0, tiled=True)
    return arrived.sum(axis=0)


def flux_difference(energy, velocity, open_mask, along):
    count = energy.shape[along] - 1
    low_energy = lax.slice_in_dim(energy, 0, count, axis=along)
    high_energy = lax.slice_in_dim(energy, 1, count + 1, axis=along)
    face_speed = 0.5 * (
        lax.slice_in_dim(velocity, 0, count, axis=along)
        + lax.slice_in_dim(velocity, 1, count + 1, axis=along)
    )
    face_open = lax.slice_in_dim(open_mask, 0, count, axis=along) * lax.slice_in_dim(
        open_mask, 1, count + 1, axis=along
    )
    flux = face_open * (
        jnp.maximum(face_speed, 0.0) * low_energy + jnp.minimum(face_speed, 0.0) * high_energy
    )
    return lax.slice_in_dim(flux, 1, count, axis=along) - lax.slice_in_dim(
        flux, 0, count - 1, axis=along
    )


def source_terms(
    flat_energy, wind_here, ice_here, cosine_dir, sine_dir, ratios, dir_here, freq_count
):
    point_count = flat_energy.shape[1]
    energy = flat_energy.reshape(dir_here, freq_count, point_count)
    ratio_square = ratios * ratios
    ratio_cube = ratio_square * ratios
    moment_band = jnp.sum(energy * ratio_square[None, :, None], axis=(0, 1))
    moment = lax.psum(moment_band, "dir")
    steepness = STEEP_COEF * moment
    damping = DAMP_RATE * steepness / (1.0 + steepness)
    wind_gain = (
        WIND_GROWTH
        * (1.0 - ice_here)[None, :]
        * jnp.maximum(
            wind_here[0][None, :] * cosine_dir[:, None] + wind_here[1][None, :] * sine_dir[:, None],
            0.0,
        )
    )
    growth = ratios[None, :, None] * (wind_gain - damping[None, :])[:, None, :]
    updated = energy * (1.0 + growth)
    stress_dir = jnp.sum(ratio_square[None, :, None] * wind_gain[:, None, :] * energy, axis=1)
    stokes_dir = jnp.sum(ratio_cube[None, :, None] * updated, axis=1)
    partial_value = jnp.stack(
        [
            STRESS_SCALE * jnp.sum(cosine_dir[:, None] * stress_dir, axis=0),
            STRESS_SCALE * jnp.sum(sine_dir[:, None] * stress_dir, axis=0),
            STOKES_SCALE * jnp.sum(cosine_dir[:, None] * stokes_dir, axis=0),
            STOKES_SCALE * jnp.sum(sine_dir[:, None] * stokes_dir, axis=0),
        ]
    )
    return (updated.reshape(dir_here * freq_count, point_count), partial_value)


def on_device(spectrum, group_speed, ocean_current, route_slot, wind_vector, ice_cover):
    blocks = lax.axis_size(BLK)
    band_count = lax.axis_size("dir")
    dir_here, freq_count, rows_here, width_y = spectrum.shape
    cell_count = rows_here * width_y
    capacity = cell_count // blocks
    bin_count = dir_here * freq_count
    currents = two_step_exchange(ocean_current, (("blk_0", "blk_1"), "blk_2"), (1, 0), 2, 1)
    currents = jnp.transpose(currents, (0, 2, 1))
    sea_mask = (route_slot >= 0).astype(jnp.float32)
    stacked = jnp.concatenate(
        [spectrum.reshape(bin_count, rows_here, width_y), group_speed, currents, sea_mask[None]],
        axis=0,
    )
    padded = with_halo(stacked, ((BLK, 1),), 1)
    energy_x = padded[:bin_count].reshape(dir_here, freq_count, rows_here + 2, width_y)
    speed_x = padded[bin_count : bin_count + freq_count]
    flow_x = padded[bin_count + freq_count]
    mask_x = padded[bin_count + freq_count + 2]
    global_dir = (lax.axis_index("dir") * dir_here + jnp.arange(dir_here, dtype=jnp.int32)).astype(
        jnp.float32
    )
    angles = 2.0 * jnp.pi * global_dir / (dir_here * band_count)
    cosine_dir = jnp.cos(angles)
    sine_dir = jnp.sin(angles)
    ratios = jnp.power(
        jnp.float32(RATIO_STEP), jnp.arange(freq_count, dtype=jnp.float32) - (freq_count - 1)
    )
    velocity_x = speed_x[None] * cosine_dir[:, None, None, None] + flow_x[None, None]
    div_x = flux_difference(
        energy_x, velocity_x, jnp.broadcast_to(mask_x[None, None], energy_x.shape), 2
    )
    velocity_y = group_speed[None] * sine_dir[:, None, None, None] + currents[1][None, None]
    widths = ((0, 0), (0, 0), (0, 0), (1, 1))
    energy_y = jnp.pad(spectrum, widths)
    mask_y = jnp.broadcast_to(jnp.pad(sea_mask, ((0, 0), (1, 1)))[None, None], energy_y.shape)
    div_y = flux_difference(energy_y, jnp.pad(velocity_y, widths), mask_y, 3)
    moved = sea_mask[None, None] * (spectrum - COURANT * (div_x + div_y))
    flat = moved.reshape(bin_count, cell_count)
    slot_index = jnp.where(route_slot >= 0, route_slot, cell_count).reshape(cell_count)
    wind_back, ice_back = in_one_piece(
        (wind_vector[0].reshape(2, blocks, capacity), ice_cover.reshape(1, blocks, capacity)),
        BLK,
        1,
        1,
        0,
    )
    wind_geo = jnp.take(
        wind_back.reshape(2, cell_count), slot_index, axis=1, mode="fill", fill_value=0.0
    )
    ice_geo = jnp.take(
        ice_back.reshape(1, cell_count), slot_index, axis=1, mode="fill", fill_value=0.0
    )
    result, partial_geo = source_terms(
        flat, wind_geo, ice_geo[0], cosine_dir, sine_dir, ratios, dir_here, freq_count
    )
    own_share = 4 // band_count
    own_parts = summed_on_arrival(partial_geo, "dir", 0)
    ocean_grid = jnp.transpose(own_parts.reshape(own_share, rows_here, width_y), (0, 2, 1))
    ocean_part = lax.all_to_all(ocean_grid, BLK, split_axis=1, concat_axis=2, tiled=True)
    return (result.reshape(dir_here, freq_count, rows_here, width_y), ocean_part)


def solution(mesh):
    finer = Mesh(
        mesh.devices.reshape(8, 8, 2, mesh.shape["dir"]), ("blk_0", "blk_1", "blk_2", "dir")
    )
    return jax.shard_map(
        on_device,
        mesh=finer,
        in_specs=(
            P("dir", None, BLK, None),
            P(None, BLK, None),
            P(None, BLK, None),
            P(BLK, None),
            P(BLK, None, None),
            P(BLK, None),
        ),
        out_specs=(P("dir", None, BLK, None), P("dir", BLK, None)),
        check_vma=False,
    )
```

profile of v0, /device:TPU:1, one launch (start us, length us, event | category | flops | bytes accessed | tf_op | source)
XLA Modules:
  0.0 142.0 jit_solution(12757614298801964621)
XLA Ops:
  0.7 0.9 reduce.8
  1.9 10.2 %all_to_all.32 = f32[2,1,2048]{2,1,0:T(1,128)S(1)} all-to-all(f32[2,1,2048]{2,1,0:T(1,128)S(1)} %reshape.402), channel_id=1, replica_groups=mesh['blk_0'=8,'blk_1'=8,'blk_2'=2,'dir'=4] {'blk_2'}, dimensions={0} | all-to-all | bytes 32768 | tf_op jit(solution)/shard_map/all_to_all | solution.py:35
  14.1 11.0 %all-to-all-start.1 = ((f32[64,2,2,1,16]{4,1,2,3,0:T(2,128)}), f32[64,2,2,1,16]{4,1,2,3,0:T(2,128)S(1)}, u32[]{:S(2)}, u32[]{:S(2)}) async-start(f32[64,2,2,1,16]{4,1,2,3,0:T(2,128)} %copy.26), calls=%async_computation.1 | async-start | bytes 262144 | tf_op jit(solution)/shard_map/all_to_all | solution.py:35
  27.8 1.4 reduce.23
  31.1 5.6 %all-to-all-done.1 = f32[64,2,2,1,16]{4,1,2,3,0:T(2,128)S(1)} async-done(((f32[64,2,2,1,16]{4,1,2,3,0:T(2,128)}), f32[64,2,2,1,16]{4,1,2,3,0:T(2,128)S(1)}, u32[]{:S(2)}, u32[]{:S(2)}) %all-to-all-start.1) | async-done | bytes 16416 | tf_op jit(solution)/shard_map/all_to_all | solution.py:35
  36.6 8.5 %all-to-all-start.2 = ((f32[3,128,16]{2,0,1:T(4,128)}), f32[3,128,16]{2,0,1:T(4,128)}, u32[]{:S(2)}, u32[]{:S(2)}) async-start(f32[3,128,16]{2,0,1:T(4,128)} %copy.30), calls=%async_computation.2 | async-start | bytes 524288 | tf_op jit(solution)/shard_map/all_to_all | solution.py:61
  45.3 2.0 %pad_maximum_fusion.10 = (f32[363,1,128]{2,1,0:T(1,128)}, f32[363,1,128]{2,1,0:T(1,128)}) fusion(f32[1,16,128]{2,1,0:T(8,128)S(1)} %get-tuple-element.17, f32[2,16,128]{2,1,0:T(8,128)S(1)} %copy.28, f32[36,16,128]{2,1,0:T(8,128)} %param.7, f32[324,16,128]{2,1,0:T(8,128)S(1)} %bitcast.50), kind=kLoop, calls=%fused_computation.43 | loop fusion | flops 278784 | bytes 3345408 | tf_op jit(solution)/shard_map/slice | solution.py:50
  47.3 3.5 %collective-permute-start = (f32[363,1,128]{2,1,0:T(1,128)}, f32[363,1,128]{2,1,0:T(1,128)S(1)}, u32[]{:S(2)}, u32[]{:S(2)}) collective-permute-start(f32[363,1,128]{2,1,0:T(1,128)} %get-tuple-element.15), channel_id=1, source_target_pairs={{0,4},{4,8},{8,12},{12,16},{16,20},{20,24},{24,28},{28,32},{32,36}... | collective-permute-start | bytes 557576 | tf_op jit(solution)/shard_map/ppermute | solution.py:52
  50.9 1.9 %collective-permute-start.1 = (f32[363,1,128]{2,1,0:T(1,128)}, f32[363,1,128]{2,1,0:T(1,128)S(1)}, u32[]{:S(2)}, u32[]{:S(2)}) collective-permute-start(f32[363,1,128]{2,1,0:T(1,128)} %get-tuple-element.16), channel_id=1, source_target_pairs={{4,0},{8,4},{12,8},{16,12},{20,16},{24,20},{28,24},{32,28},{36,32}... | collective-permute-start | bytes 557576 | tf_op jit(solution)/shard_map/ppermute | solution.py:53
  53.2 4.5 %fusion.4 = f32[9,36,16,129]{3,2,1,0:T(8,128)} fusion(f32[9,36,16,128]{3,2,1,0:T(8,128)S(1)} %copy-done, f32[9,36,16,128]{3,2,1,0:T(8,128)S(1)} %multiply_add_fusion.1, f32[16,129]{1,0:T(8,128)S(1)} %fusion.13), kind=kLoop, calls=%fused_computation.10 | loop fusion | flops 5349888 | bytes 7991616 | tf_op jit(solution)/shard_map/mul | solution.py:82
  57.7 2.5 %all-to-all-done.2 = f32[3,128,16]{2,0,1:T(4,128)} async-done(((f32[3,128,16]{2,0,1:T(4,128)}), f32[3,128,16]{2,0,1:T(4,128)}, u32[]{:S(2)}, u32[]{:S(2)}) %all-to-all-start.2) | async-done | bytes 24608 | tf_op jit(solution)/shard_map/all_to_all | solution.py:61
  60.2 1.0 split.9
  61.2 1.8 %copy.31 = f32[2,128,16]{0,2,1:T(8,128)} copy(f32[2,128,16]{2,0,1:T(2,128)S(1)} %split.9) | data formatting | bytes 32768 | tf_op jit(solution)/shard_map/split | solution.py:62
  63.0 8.8 %gather_fusion.1 = f32[2048,2]{1,0:T(8,128)} fusion(f32[2,2048]{0,1:T(8,128)} %bitcast.58, s32[2048]{0:T(1024)S(1)} %broadcast_clamp_fusion), kind=kCustom, calls=%fused_computation.1 | custom fusion | bytes 40960 | tf_op jit(solution)/shard_map/jit(_take)/gather | solution.py:171
  71.8 1.6 %select_bitcast_fusion = f32[2,2048]{0,1:T(8,128)S(1)} fusion(f32[2048,2]{1,0:T(8,128)} %gather_fusion.1, pred[2048]{0:T(1024)(128)(4,1)S(1)} %compare_and_fusion), kind=kLoop, calls=%fused_computation.37 | loop fusion | flops 4096 | bytes 34816 | tf_op jit(solution)/shard_map/jit(_take)/select_n | solution.py:171
  73.4 0.9 slice_reduce_fusion.1
  74.3 1.2 slice_reduce_fusion.2
  75.5 11.8 %gather_fusion = f32[2048]{0:T(1024)S(1)} fusion(f32[2048]{0:T(1024)S(1)} %reshape.358, s32[2048]{0:T(1024)S(1)} %broadcast_clamp_fusion), kind=kCustom, calls=%fused_computation | custom fusion | bytes 24576 | tf_op jit(solution)/shard_map/jit(_take)/gather | solution.py:174
  88.7 1.6 %fusion.7 = f32[9,36,17,128]{3,2,1,0:T(8,128)S(1)} fusion(f32[9,36,18,128]{3,2,1,0:T(8,128)S(1)} %bitcast.55, f32[9,36,18,128]{3,2,1,0:T(8,128)S(1)} %multiply_add_fusion, f32[17,128]{1,0:T(8,128)S(1)} %fusion.15), kind=kLoop, calls=%fused_computation.14 | loop fusion | flops 5640192 | bytes 14109184 | tf_op jit(solution)/shard_map/mul | solution.py:82
  91.1 2.7 %multiply_reduce_fusion.1 = (f32[9,16,128]{2,1,0:T(8,128)S(1)}, f32[16,128]{1,0:T(8,128)S(1)}, f32[9,36,16,128]{3,2,1,0:T(8,128)}) fusion(f32[9,16,128]{2,1,0:T(8,128)S(1)} %maximum_multiply_fusion, f32[36]{0:T(128)S(1)} %fusion.21, f32[9,36,16,128]{3,2,1,0:T(8,128)S(1)} %copy-done, f32[9,36,16,129]{3,2,1,0:T(8,128)S(1)} %bitcast.57, ...), kind=kLoop, calls=%fused_computation.31 | loop fusion | flops 7278592 | bytes 16089232 | tf_op jit(solution)/shard_map/reduce_sum | solution.py:111
  93.8 8.7 %psum.7 = f32[2048]{0:T(1024)S(1)} all-reduce(f32[2048]{0:T(1024)S(1)} %bitcast.68), channel_id=1, replica_groups=mesh['blk_0'=8,'blk_1'=8,'blk_2'=2,'dir'=4] {'dir'}, use_global_device_ids=true, to_apply=%region_1.2 | all-reduce | flops 2048 | bytes 16384 | tf_op jit(solution)/shard_map/psum | solution.py:98
  102.6 3.9 %multiply_reduce_fusion = (f32[9,16,128]{2,1,0:T(8,128)S(1)}, f32[9,36,16,128]{3,2,1,0:T(8,128)}) fusion(f32[36]{0:T(128)S(1)} %get-tuple-element.22, f32[9,36,16,128]{3,2,1,0:T(8,128)} %get-tuple-element.14, f32[9,16,128]{2,1,0:T(8,128)S(1)} %broadcast_subtract_fusion, f32[36]{0:T(128)S(1)} %get-tuple-element.21), kind=kLoop, calls=%fused_computation.30 | loop fusion | flops 3299328 | bytes 5456160 | tf_op jit(solution)/shard_map/reduce_sum | solution.py:112
  106.7 6.7 %all_to_all.33 = f32[4,1,2048]{2,1,0:T(1,128)S(1)} all-to-all(f32[4,1,2048]{2,1,0:T(1,128)S(1)} %reshape.356), channel_id=1, replica_groups=mesh['blk_0'=8,'blk_1'=8,'blk_2'=2,'dir'=4] {'dir'}, dimensions={0} | all-to-all | bytes 65536 | tf_op jit(solution)/shard_map/all_to_all | solution.py:67
  113.5 27.0 %all_to_all.34 = f32[1,128,16]{2,0,1:T(1,128)S(1)} all-to-all(f32[1,128,16]{2,0,1:T(1,128)S(1)} %copy.32), channel_id=1, replica_groups=mesh['blk_0'=8,'blk_1'=8,'blk_2'=2,'dir'=4] {'blk_0','blk_1','blk_2'}, dimensions={1} | all-to-all | bytes 16384 | tf_op jit(solution)/shard_map/all_to_all | solution.py:183
  (58 shorter events, 11.4 us)
Async XLA Ops:
  0.6 44.7 %copy-start = (f32[9,36,16,128]{3,2,1,0:T(8,128)S(1)}, f32[9,36,16,128]{3,2,1,0:T(8,128)}, u32[]{:S(2)}) copy-start(f32[9,36,16,128]{3,2,1,0:T(8,128)} %param.6) | copy-start | bytes 7962628
  0.6 52.2 %copy-start.1 = (f32[36,16,128]{2,1,0:T(8,128)S(1)}, f32[36,16,128]{2,1,0:T(8,128)}, u32[]{:S(2)}) copy-start(f32[36,16,128]{2,1,0:T(8,128)} %param.7) | copy-start | bytes 884740
  14.1 22.5 %all-to-all-start.1 = ((f32[64,2,2,1,16]{4,1,2,3,0:T(2,128)}), f32[64,2,2,1,16]{4,1,2,3,0:T(2,128)S(1)}, u32[]{:S(2)}, u32[]{:S(2)}) async-start(f32[64,2,2,1,16]{4,1,2,3,0:T(2,128)} %copy.26), calls=%async_computation.1 | async-start | bytes 262144 | tf_op jit(solution)/shard_map/all_to_all | solution.py:35
  36.6 23.6 %all-to-all-start.2 = ((f32[3,128,16]{2,0,1:T(4,128)}), f32[3,128,16]{2,0,1:T(4,128)}, u32[]{:S(2)}, u32[]{:S(2)}) async-start(f32[3,128,16]{2,0,1:T(4,128)} %copy.30), calls=%async_computation.2 | async-start | bytes 524288 | tf_op jit(solution)/shard_map/all_to_all | solution.py:61
  47.3 40.1 %collective-permute-start = (f32[363,1,128]{2,1,0:T(1,128)}, f32[363,1,128]{2,1,0:T(1,128)S(1)}, u32[]{:S(2)}, u32[]{:S(2)}) collective-permute-start(f32[363,1,128]{2,1,0:T(1,128)} %get-tuple-element.15), channel_id=1, source_target_pairs={{0,4},{4,8},{8,12},{12,16},{16,20},{20,24},{24,28},{28,32},{32,36}... | collective-permute-start | bytes 557576 | tf_op jit(solution)/shard_map/ppermute | solution.py:52
  50.9 36.6 %collective-permute-start.1 = (f32[363,1,128]{2,1,0:T(1,128)}, f32[363,1,128]{2,1,0:T(1,128)S(1)}, u32[]{:S(2)}, u32[]{:S(2)}) collective-permute-start(f32[363,1,128]{2,1,0:T(1,128)} %get-tuple-element.16), channel_id=1, source_target_pairs={{4,0},{8,4},{12,8},{16,12},{20,16},{24,20},{28,24},{32,28},{36,32}... | collective-permute-start | bytes 557576 | tf_op jit(solution)/shard_map/ppermute | solution.py:53
  75.5 11.8 %copy-start.2 = (s32[16,128]{1,0:T(8,128)S(1)}, s32[16,128]{1,0:T(8,128)}, u32[]{:S(2)}) copy-start(s32[16,128]{1,0:T(8,128)} %param.9) | copy-start | bytes 24580
  88.6 2.2 %slice-start = ((s8[5308416]{0:T(1024)(128)(4,1)}), s8[4194304]{0:T(1024)(128)(4,1)S(1)}, s32[]{:S(2)}) async-start(s8[5308416]{0:T(1024)(128)(4,1)} %bitcast.56), calls=%async_computation.5 | async-start | bytes 8388608
  88.6 2.5 %slice-start.1 = ((s8[5308416]{0:T(1024)(128)(4,1)}), s8[1114112]{0:T(1024)(128)(4,1)S(1)}, s32[]{:S(2)}) async-start(s8[5308416]{0:T(1024)(128)(4,1)} %bitcast.56), calls=%async_computation.6 | async-start | bytes 2228224
where the time goes:
time: 143 us; the launch traced here: 142 us
  blocking collectives  52.6 us (37%)
  local copies, waits for them, and re-layouts  31.2 us (22%)
  starting transfers between devices  24.9 us (17%)
  other arithmetic  24.1 us (17%)
  waiting for transfers between devices  8.13 us (6%)
    all_to_all x1, blocking collectives, on_device(): lax.all_to_all(ocean_grid, BLK, split_axis=1, concat_axis=2, tiled=True)  27 us
    gather x1, local copies, waits for them, and re-layouts, on_device(): jnp.take(ice_back.reshape(1, cell_count), slot_index, axis=1, mode='fill'...  11.8 us
    all_to_all x1, starting transfers between devices, turned_blocks(): filled = lax.all_to_all(filled, axes[k], k, k, tiled=True)  11 us
    all_to_all x1, blocking collectives, turned_blocks(): filled = lax.all_to_all(filled, axes[k], k, k, tiled=True)  10.2 us
    gather x1, local copies, waits for them, and re-layouts, on_device(): jnp.take(wind_back.reshape(2, cell_count), slot_index, axis=1, mode='fill...  8.79 us
    psum x1, blocking collectives, source_terms(): moment = lax.psum(moment_band, 'dir')  8.73 us
    all_to_all x1, starting transfers between devices, in_one_piece(): lax.all_to_all(both, axis, split_axis=split_dim, concat_axis=concat_dim,...  8.52 us
    all_to_all x1, blocking collectives, summed_on_arrival(): lax.all_to_all(pieces, axis, split_axis=0, concat_axis=0, tiled=True)  6.65 us
  transfers between devices with their start and end apart: 4, of which 2 were waited for; matrix products, arithmetic and copies ran while one was open for 28% of the time, Pallas kernels for 0%

commit v1 on v0

v1 whole, which is shorter than its diff:
```python
import jax
import jax.numpy as jnp
import numpy as np
from jax import lax
from jax.experimental import pallas as pl
from jax.experimental.pallas import tpu as pltpu
from jax.sharding import PartitionSpec as P

BLK = "blk"
DIR = "dir"
VMEM = pltpu.VMEM
SMEM = pltpu.SMEM

COURANT = 0.15
WIND_GROWTH = 0.15
DAMP_RATE = 0.5
STEEP_COEF = 0.01
STOKES_SCALE = 0.15
RATIO_STEP = 1.1

LANES = 128
ROWS = 16
CUR_X, CUR_Y, WIND_X, WIND_Y, ICE = 0, 24, 48, 64, 80


def vmem_specs(count):
    return [pl.BlockSpec(memory_space=VMEM)] * count


def lane_of(shape):
    return lax.broadcasted_iota(jnp.int32, shape, len(shape) - 1)


def message_kernel(cur_ref, wind_ref, ice_ref, out_ref, x_ref):
    for c in range(2):
        for r in range(ROWS):
            x_ref[c, r : r + 1, :] = wind_ref[c : c + 1, LANES * r : LANES * (r + 1)]
    lane = lane_of((ROWS, LANES))

    def put(s, values, start):
        return pltpu.roll(values, (start - ROWS * s) % LANES, 1)

    for s in range(8):
        row = jnp.where(lane < CUR_Y, put(s, cur_ref[0], CUR_X + 1), put(s, cur_ref[1], CUR_Y))
        row = jnp.where(lane < WIND_X, row, put(s, x_ref[0], WIND_X))
        row = jnp.where(lane < WIND_Y, row, put(s, x_ref[1], WIND_Y))
        row = jnp.where(lane < ICE, row, put(s, ice_ref[...], ICE))
        out_ref[pl.ds(s, ROWS, stride=8), :] = row
    whole = out_ref[...]
    wide = lane_of((LANES, LANES))
    before = pltpu.roll(pltpu.roll(whole, 1, 0), LANES - ROWS, 1)
    after = pltpu.roll(pltpu.roll(whole, LANES - 1, 0), ROWS, 1)
    whole = jnp.where(wide == CUR_X, before, whole)
    out_ref[...] = jnp.where(wide == CUR_X + ROWS + 1, after, whole)


def edge_kernel(bins, freqs, spec_ref, speed_ref, slot_ref, last_ref, first_ref):
    for out_ref, row in ((last_ref, ROWS - 1), (first_ref, 0)):
        out_ref[0:bins, :] = spec_ref[pl.ds(row, bins, stride=ROWS), :]
        out_ref[bins : bins + freqs, :] = speed_ref[pl.ds(row, freqs, stride=ROWS), :]
        sea = jnp.where(slot_ref[row : row + 1, :] >= 0, 1.0, 0.0)
        out_ref[bins + freqs :, :] = jnp.broadcast_to(sea, (8, LANES))


def move_kernel(
    dirs,
    freqs,
    at_ref,
    trig_ref,
    got_ref,
    spec_ref,
    speed_ref,
    low_ref,
    high_ref,
    slot_ref,
    moved_ref,
    parts_ref,
    cell_ref,
    turned_ref,
    sx_ref,
    sy_ref,
    s16_ref,
    f16_ref,
):
    shape = (ROWS, LANES)
    row, lane = lax.broadcasted_iota(jnp.int32, shape, 0), lane_of(shape)
    bins = dirs * freqs
    turned_ref[...] = got_ref[...].T

    def shifted_down(values, first):
        return jnp.where(row == 0, jnp.broadcast_to(first, shape), pltpu.roll(values, 1, 0))

    def next_y(values):
        return pltpu.roll(values, LANES - 1, 1)

    slots = slot_ref[...]
    sea = jnp.where(slots >= 0, 1.0, 0.0)
    sea_low, sea_high = low_ref[bins + freqs : bins + freqs + 1, :], high_ref[bins + freqs : bins + freqs + 1, :]
    half = 0.5 * COURANT
    open_x = half * sea * shifted_down(sea, sea_low)
    open_y = jnp.where(lane < LANES - 1, half * sea * next_y(sea), 0.0)
    open_16 = half * sea[ROWS - 1 : ROWS, :] * sea_high
    flow_x = open_x * (turned_ref[CUR_X : CUR_X + ROWS, :] + turned_ref[CUR_X + 1 : CUR_X + ROWS + 1, :])
    flow_16 = open_16 * (turned_ref[CUR_X + ROWS : CUR_X + ROWS + 1, :] + turned_ref[CUR_X + ROWS + 1 : CUR_X + ROWS + 2, :])
    cur_y = turned_ref[CUR_Y : CUR_Y + ROWS, :]
    flow_y = open_y * (cur_y + next_y(cur_y))

    owner, place = jnp.maximum(slots, 0) // 16, jnp.where(slots >= 0, slots % 16, -1)
    wind_x, wind_y, ice = (jnp.zeros(shape, jnp.float32) for _ in range(3))
    for s in range(16):
        here = place == s

        def picked(start, old):
            table = jnp.broadcast_to(turned_ref[start + s : start + s + 1, :], shape)
            return jnp.where(here, jnp.take_along_axis(table, owner, axis=1), old)

        wind_x, wind_y, ice = picked(WIND_X, wind_x), picked(WIND_Y, wind_y), picked(ICE, ice)
    gain = WIND_GROWTH * (1.0 - ice)
    cell_ref[0:16, :] = wind_x
    cell_ref[16:32, :] = wind_y
    cell_ref[32:48, :] = gain

    def faces(k, _):
        base = pl.multiple_of(k * ROWS, ROWS)
        speed = speed_ref[pl.ds(base, ROWS), :]
        sx_ref[pl.ds(base, ROWS), :] = open_x * (speed + shifted_down(speed, low_ref[pl.ds(bins + k, 1), :]))
        sy_ref[pl.ds(base, ROWS), :] = open_y * (speed + next_y(speed))
        return 0

    lax.fori_loop(0, freqs, faces, 0, unroll=4)
    s16_ref[...] = open_16 * (speed_ref[pl.ds(ROWS - 1, freqs, stride=ROWS), :] + high_ref[bins : bins + freqs, :])

    zero = jnp.zeros(shape, jnp.float32)
    moment, stress_x, stress_y, drift_x, drift_y, damp_x, damp_y = (zero,) * 7
    at = at_ref[0]
    for j in range(dirs):
        cosine, sine = trig_ref[at, j], trig_ref[at, dirs + j]
        face = s16_ref[...] * cosine + flow_16
        f16_ref[...] = face * jnp.where(
            face > 0.0,
            spec_ref[pl.ds(j * freqs * ROWS + ROWS - 1, freqs, stride=ROWS), :],
            high_ref[j * freqs : (j + 1) * freqs, :],
        )

        def step(k, sums):
            second, third, fourth = sums
            base = pl.multiple_of(k * ROWS, ROWS)
            here = pl.multiple_of(j * freqs * ROWS + k * ROWS, ROWS)
            energy = spec_ref[pl.ds(here, ROWS), :]
            u = sx_ref[pl.ds(base, ROWS), :] * cosine + flow_x
            below = u * jnp.where(u > 0.0, shifted_down(energy, low_ref[pl.ds(j * freqs + k, 1), :]), energy)
            above = jnp.where(
                row == ROWS - 1, jnp.broadcast_to(f16_ref[pl.ds(k, 1), :], shape), pltpu.roll(below, ROWS - 1, 0)
            )
            v = sy_ref[pl.ds(base, ROWS), :] * sine + flow_y
            right = v * jnp.where(v > 0.0, energy, next_y(energy))
            left = pltpu.roll(right, 1, 1)
            moved = sea * (energy - ((above - below) + (right - left)))
            moved_ref[pl.ds(here, ROWS), :] = moved
            return (
                second * (RATIO_STEP**-2) + moved,
                third * (RATIO_STEP**-3) + moved,
                fourth * (RATIO_STEP**-4) + moved,
            )

        second, third, fourth = lax.fori_loop(0, freqs, step, (zero, zero, zero), unroll=4)
        wind_gain = gain * jnp.maximum(wind_x * cosine + wind_y * sine, 0.0)
        push = wind_gain * second
        drift = third + wind_gain * fourth
        moment += second
        stress_x += cosine * push
        stress_y += sine * push
        drift_x += cosine * drift
        drift_y += sine * drift
        damp_x += cosine * fourth
        damp_y += sine * fourth
    for c, (main, damped) in enumerate(((stress_x, zero), (stress_y, zero), (drift_x, damp_x), (drift_y, damp_y))):
        parts_ref[c, 0:16, :] = moment
        parts_ref[c, 16:32, :] = main
        parts_ref[c, 32:48, :] = damped


def forcing_kernel(at_ref, parts_ref, damping_ref, out_ref):
    parts = (parts_ref[0] + parts_ref[1]) + (parts_ref[2] + parts_ref[3])
    steepness = STEEP_COEF * parts[0:16]
    damping = DAMP_RATE * steepness / (1.0 + steepness)
    damping_ref[...] = damping
    own = parts[16:32] - damping * parts[32:48]
    own = jnp.where(at_ref[0] < 2, 1.0, STOKES_SCALE) * own
    out_ref[...] = jnp.concatenate([own, jnp.zeros((LANES - ROWS, LANES), jnp.float32)], axis=0).T


def update_kernel(dirs, freqs, at_ref, trig_ref, moved_ref, cell_ref, damping_ref, out_ref):
    j, at = pl.program_id(0), at_ref[0]
    cosine, sine = trig_ref[at, j], trig_ref[at, dirs + j]
    wind = jnp.maximum(cell_ref[0:16, :] * cosine + cell_ref[16:32, :] * sine, 0.0)
    growth = cell_ref[32:48, :] * wind - damping_ref[...]
    start = pl.multiple_of(j * freqs * ROWS, ROWS)
    for k in range(freqs):
        ratio = RATIO_STEP ** (k - freqs + 1)
        out_ref[k * ROWS : (k + 1) * ROWS, :] = moved_ref[pl.ds(start + k * ROWS, ROWS), :] * (1.0 + ratio * growth)


def row_kernel(got_ref, out_ref):
    lane = lane_of((ROWS, LANES))
    row = got_ref[pl.ds(0, ROWS, stride=8), :]
    for s in range(1, 8):
        row = jnp.where(lane < ROWS * s, row, pltpu.roll(got_ref[pl.ds(s, ROWS, stride=8), :], ROWS * s, 1))
    out_ref[...] = row


def f32(*shape):
    return jax.ShapeDtypeStruct(shape, jnp.float32)


def on_device(spectrum, group_speed, ocean_current, route_slot, wind_vector, ice_cover):
    dirs, freqs, _, _ = spectrum.shape
    bands, blocks = lax.axis_size(DIR), lax.axis_size(BLK)
    bins = dirs * freqs
    at = lax.axis_index(DIR).astype(jnp.int32).reshape(1)
    angles = (2.0 * np.pi * np.arange(bands * dirs, dtype=np.float32) / np.float32(bands * dirs)).astype(np.float32)
    angles = angles.astype(np.float64).reshape(bands, dirs)
    trig = jnp.asarray(np.concatenate([np.cos(angles), np.sin(angles)], axis=1).astype(np.float32))
    smem = pl.BlockSpec(memory_space=SMEM)

    messages = pl.pallas_call(
        message_kernel,
        out_shape=f32(LANES, LANES),
        in_specs=vmem_specs(3),
        out_specs=vmem_specs(1)[0],
        scratch_shapes=[VMEM((2, ROWS, LANES), jnp.float32)],
        name="messages",
    )(
        ocean_current.reshape(2, ROWS, LANES),
        wind_vector.reshape(2, ROWS * LANES),
        ice_cover.reshape(ROWS, LANES),
    )
    got = lax.all_to_all(messages, BLK, 0, 0, tiled=True)

    flat = spectrum.reshape(bins * ROWS, LANES)
    speed = group_speed.reshape(freqs * ROWS, LANES)
    edge = f32(bins + freqs + 8, LANES)
    last, first = pl.pallas_call(
        lambda *refs: edge_kernel(bins, freqs, *refs),
        out_shape=(edge, edge),
        in_specs=vmem_specs(3),
        out_specs=tuple(vmem_specs(2)),
        name="edges",
    )(flat, speed, route_slot)
    up = [(i, i + 1) for i in range(blocks - 1)]
    low = lax.ppermute(last, BLK, up)
    high = lax.ppermute(first, BLK, [(j, i) for i, j in up])

    moved, parts, cell = pl.pallas_call(
        lambda *refs: move_kernel(dirs, freqs, *refs),
        out_shape=(f32(bins * ROWS, LANES), f32(bands, 48, LANES), f32(48, LANES)),
        in_specs=[smem, smem] + vmem_specs(6),
        out_specs=tuple(vmem_specs(3)),
        scratch_shapes=[
            VMEM((LANES, LANES), jnp.float32),
            VMEM((freqs * ROWS, LANES), jnp.float32),
            VMEM((freqs * ROWS, LANES), jnp.float32),
            VMEM((freqs, LANES), jnp.float32),
            VMEM((freqs, LANES), jnp.float32),
        ],
        name="move",
    )(at, trig, got, flat, speed, low, high, route_slot)

    parts = lax.all_to_all(parts, DIR, 0, 0, tiled=True)
    damping, own = pl.pallas_call(
        forcing_kernel,
        out_shape=(f32(ROWS, LANES), f32(LANES, LANES)),
        in_specs=[smem] + vmem_specs(1),
        out_specs=tuple(vmem_specs(2)),
        name="forcing",
    )(at, parts)
    ocean = lax.all_to_all(own, BLK, 0, 0, tiled=True)
    result = pl.pallas_call(
        lambda *refs: update_kernel(dirs, freqs, *refs),
        out_shape=f32(bins * ROWS, LANES),
        grid=(dirs,),
        in_specs=[smem, smem] + vmem_specs(3),
        out_specs=pl.BlockSpec((freqs * ROWS, LANES), lambda j: (j, 0)),
        name="update",
        cost_estimate=pl.CostEstimate(flops=3 * bins * ROWS * LANES, bytes_accessed=8 * bins * ROWS * LANES, transcendentals=0),
    )(at, trig, moved, cell, damping)
    ocean = pl.pallas_call(
        row_kernel,
        out_shape=f32(ROWS, LANES),
        in_specs=vmem_specs(1),
        out_specs=vmem_specs(1)[0],
        name="rows",
    )(ocean)
    return (result.reshape(spectrum.shape), ocean.reshape(1, 1, ROWS * LANES))


def solution(mesh):
    return jax.shard_map(
        on_device,
        mesh=mesh,
        in_specs=(
            P(DIR, None, BLK, None),
            P(None, BLK, None),
            P(None, BLK, None),
            P(BLK, None),
            P(BLK, None, None),
            P(BLK, None),
        ),
        out_specs=(P(DIR, None, BLK, None), P(DIR, BLK, None)),
        check_vma=False,
    )
```

time: 143 us -> 91.3 us (0.64)
  blocking collectives: 52.6 us -> 8.77 us
  Pallas kernels: 0 us -> 30.2 us
  local copies, waits for them, and re-layouts: 31.2 us -> 1.37 us
  other arithmetic: 24.1 us -> 0 us
  waiting for transfers between devices: 8.13 us -> 17.4 us
  starting transfers between devices: 24.9 us -> 32.3 us
    all_to_all x3 -> x1, blocking collectives: 43.8 us -> 8.77 us  [on_device(): parts = lax.all_to_all(parts, DIR, 0, 0, tiled=True)]
    pallas_call x0 -> x6, Pallas kernels: none -> 30.2 us  [the longest x1 17.1 us: on_device(): pl.pallas_call(lambda *refs: move_kernel(dirs, freqs, *refs), out_shape=(...]
    gather x2 -> x0, local copies, waits for them, and re-layouts: 20.6 us -> none  [the longest x1 11.8 us: on_device(): jnp.take(ice_back.reshape(1, cell_count), slot_index, axis=1, mode='fill'...]
    all_to_all x2, waiting for transfers between devices: 8.12 us -> 17.4 us  [the longest x1 11.5 us: on_device(): got = lax.all_to_all(messages, BLK, 0, 0, tiled=True)]
    psum x1 -> x0, blocking collectives: 8.73 us -> none  [source_terms(): moment = lax.psum(moment_band, 'dir')]
    reduce_sum x4 -> x0, other arithmetic: 6.65 us -> none  [the longest x1 3.87 us: source_terms(): stokes_dir = jnp.sum(ratio_cube[None, :, None] * updated, axis=1)]
    mul x9 -> x0, other arithmetic: 6.32 us -> none  [the longest x2 6.12 us: flux_difference(): face_open * (jnp.maximum(face_speed, 0.0) * low_energy + jnp.minimum(face...]
    ppermute x2, starting transfers between devices: 5.45 us -> 10 us  [the longest x1 5.46 us: on_device(): high = lax.ppermute(first, BLK, [(j, i) for i, j in up])]
  transfers between devices with their start and end apart: 4 -> 4, of which waited for: 2 -> 2; matrix products, arithmetic and copies ran while one was open for 28% -> 0% of each run, Pallas kernels for 0% -> 8%
where the time goes in v1:
time: 91.3 us; the launch traced here: 90.7 us
  starting transfers between devices  32.3 us (35%)
  Pallas kernels  30.2 us (33%)
  waiting for transfers between devices  17.4 us (19%)
  blocking collectives  8.77 us (10%)
  local copies, waits for them, and re-layouts  1.37 us (2%)
    pallas_call x1, Pallas kernels, on_device(): pl.pallas_call(lambda *refs: move_kernel(dirs, freqs, *refs), out_shape=(...  17.1 us
    all_to_all x1, starting transfers between devices, on_device(): got = lax.all_to_all(messages, BLK, 0, 0, tiled=True)  15.1 us
    all_to_all x1, waiting for transfers between devices, on_device(): got = lax.all_to_all(messages, BLK, 0, 0, tiled=True)  11.5 us
    all_to_all x1, blocking collectives, on_device(): parts = lax.all_to_all(parts, DIR, 0, 0, tiled=True)  8.77 us
    all_to_all x1, starting transfers between devices, on_device(): ocean = lax.all_to_all(own, BLK, 0, 0, tiled=True)  7.11 us
    all_to_all x1, waiting for transfers between devices, on_device(): ocean = lax.all_to_all(own, BLK, 0, 0, tiled=True)  5.97 us
    pallas_call x1, Pallas kernels, on_device(): pl.pallas_call(lambda *refs: update_kernel(dirs, freqs, *refs), out_shape...  5.64 us
    ppermute x1, starting transfers between devices, on_device(): high = lax.ppermute(first, BLK, [(j, i) for i, j in up])  5.46 us
  transfers between devices with their start and end apart: 4, of which 2 were waited for; matrix products, arithmetic and copies ran while one was open for 0% of the time, Pallas kernels for 8%

profile of v1, /device:TPU:1, one launch (start us, length us, event | category | flops | bytes accessed | tf_op | source)
XLA Modules:
  0.0 90.7 jit_solution(5742861303003571898)
XLA Ops:
  0.6 2.7 %edges.1 = (f32[368,128]{1,0:T(8,128)}, f32[368,128]{1,0:T(8,128)}) custom-call(f32[5184,128]{1,0:T(8,128)} %bitcast.16, f32[576,128]{1,0:T(8,128)} %bitcast.19, s32[16,128]{1,0:T(8,128)} %refs_7_.1), custom_call_target="tpu_custom_call" | custom-call | tf_op jit(solution)/shard_map/edges/pallas_call | solution.py:243
  3.3 4.6 %collective-permute-start = (f32[368,128]{1,0:T(8,128)}, f32[368,128]{1,0:T(8,128)S(1)}, u32[]{:S(2)}, u32[]{:S(2)}) collective-permute-start(f32[368,128]{1,0:T(8,128)} %get-tuple-element.9), channel_id=1, source_target_pairs={{0,4},{4,8},{8,12},{12,16},{16,20},{20,24},{24,28},{28,32},{32,36}... | collective-permute-start | bytes 565256 | tf_op jit(solution)/shard_map/ppermute | solution.py:251
  7.9 5.5 %collective-permute-start.1 = (f32[368,128]{1,0:T(8,128)}, f32[368,128]{1,0:T(8,128)S(1)}, u32[]{:S(2)}, u32[]{:S(2)}) collective-permute-start(f32[368,128]{1,0:T(8,128)} %get-tuple-element.10), channel_id=1, source_target_pairs={{4,0},{8,4},{12,8},{16,12},{20,16},{24,20},{28,24},{32,28},{36,32}... | collective-permute-start | bytes 565256 | tf_op jit(solution)/shard_map/ppermute | solution.py:252
  13.4 1.6 %messages.1 = f32[128,128]{1,0:T(8,128)} custom-call(f32[2,16,128]{2,1,0:T(8,128)} %bitcast.25, f32[2,2048]{1,0:T(2,128)} %bitcast.26, f32[16,128]{1,0:T(8,128)} %bitcast.28), custom_call_target="tpu_custom_call" | custom-call | tf_op jit(solution)/shard_map/messages/pallas_call | solution.py:226
  15.0 15.1 %all-to-all-start = ((f32[128,1,128]{2,1,0:T(1,128)}), f32[128,1,128]{2,1,0:T(1,128)S(1)}, u32[]{:S(2)}, u32[]{:S(2)}) async-start(f32[128,1,128]{2,1,0:T(1,128)} %bitcast.23), calls=%async_computation | async-start | bytes 131072 | tf_op jit(solution)/shard_map/all_to_all | solution.py:238
  30.2 11.5 %all-to-all-done = f32[128,1,128]{2,1,0:T(1,128)S(1)} async-done(((f32[128,1,128]{2,1,0:T(1,128)}), f32[128,1,128]{2,1,0:T(1,128)S(1)}, u32[]{:S(2)}, u32[]{:S(2)}) %all-to-all-start) | async-done | bytes 65568 | tf_op jit(solution)/shard_map/all_to_all | solution.py:238
  41.6 0.0 copy-start
  41.6 0.0 collective-permute-done.refs_5_
  41.6 0.0 copy-start.2
  41.6 0.0 collective-permute-done.1.refs_6_
  41.6 0.0 copy-start.3
  41.7 0.6 copy-done
  42.3 0.1 copy-done.2
  42.3 0.1 copy-done.3
  42.4 17.1 %move.1 = (f32[5184,128]{1,0:T(8,128)}, f32[4,48,128]{2,1,0:T(8,128)}, f32[48,128]{1,0:T(8,128)}) custom-call(s32[1]{0:T(128)} %bitcast.refs_0_.at_ref, f32[4,18]{1,0:T(4,128)} %constant.6.clone.refs_1_, f32[128,128]{1,0:T(8,128)} %bitcast.21, f32[5184,128]{1,0:T(8,128)} %bitcast.17, f32[576,128]{1,0:T(8,128)} %bitcast.20, f32[368,128]{1,0:T(8,128)} %copy-done.2, ...), custom_call_target="tpu_custom_call" | custom-call | tf_op jit(solution)/shard_map/move/pallas_call | solution.py:254
  59.5 8.8 %all_to_all.27.parts_ref = f32[4,48,128]{2,1,0:T(8,128)} all-to-all(f32[4,48,128]{2,1,0:T(8,128)} %get-tuple-element.13), channel_id=1, replica_groups=mesh['blk'=128,'dir'=4] {'dir'}, dimensions={0} | all-to-all | bytes 196608 | tf_op jit(solution)/shard_map/all_to_all | solution.py:269
  68.2 1.6 %forcing.1 = (f32[16,128]{1,0:T(8,128)}, f32[128,128]{1,0:T(8,128)}) custom-call(s32[1]{0:T(128)} %bitcast.refs_0_.at_ref, f32[4,48,128]{2,1,0:T(8,128)} %all_to_all.27.parts_ref), custom_call_target="tpu_custom_call" | custom-call | tf_op jit(solution)/shard_map/forcing/pallas_call | solution.py:270
  69.9 7.1 %all-to-all-start.2 = ((f32[128,1,128]{2,1,0:T(1,128)}), f32[128,1,128]{2,1,0:T(1,128)S(1)}, u32[]{:S(2)}, u32[]{:S(2)}) async-start(f32[128,1,128]{2,1,0:T(1,128)} %bitcast.24), calls=%async_computation.2 | async-start | bytes 131072 | tf_op jit(solution)/shard_map/all_to_all | solution.py:277
  77.0 5.6 %update.1 = f32[5184,128]{1,0:T(8,128)} custom-call(s32[1]{0:T(128)} %bitcast.refs_0_.at_ref, f32[4,18]{1,0:T(4,128)} %constant.6.clone.refs_1_, f32[5184,128]{1,0:T(8,128)} %get-tuple-element.11.refs_2_, f32[48,128]{1,0:T(8,128)} %get-tuple-element.12.refs_3_, f32[16,128]{1,0:T(8,128)} %get-tuple-element.14.refs_4_), custom_call_target="tpu_custom_call" | custom-call | flops 1990656 | bytes 5308416 | tf_op jit(solution)/shard_map/update/pallas_call | solution.py:278
  82.6 6.0 %all-to-all-done.2 = f32[128,1,128]{2,1,0:T(1,128)S(1)} async-done(((f32[128,1,128]{2,1,0:T(1,128)}), f32[128,1,128]{2,1,0:T(1,128)S(1)}, u32[]{:S(2)}, u32[]{:S(2)}) %all-to-all-start.2) | async-done | bytes 65568 | tf_op jit(solution)/shard_map/all_to_all | solution.py:277
  88.6 0.0 copy-start.1
  88.6 0.6 copy-done.1
  89.2 1.5 %rows.1 = f32[16,128]{1,0:T(8,128)} custom-call(f32[128,128]{1,0:T(8,128)} %bitcast.22), custom_call_target="tpu_custom_call" | custom-call | tf_op jit(solution)/shard_map/rows/pallas_call | solution.py:287
Async XLA Ops:
  3.3 38.3 %collective-permute-start = (f32[368,128]{1,0:T(8,128)}, f32[368,128]{1,0:T(8,128)S(1)}, u32[]{:S(2)}, u32[]{:S(2)}) collective-permute-start(f32[368,128]{1,0:T(8,128)} %get-tuple-element.9), channel_id=1, source_target_pairs={{0,4},{4,8},{8,12},{12,16},{16,20},{20,24},{24,28},{28,32},{32,36}... | collective-permute-start | bytes 565256 | tf_op jit(solution)/shard_map/ppermute | solution.py:251
  7.9 33.7 %collective-permute-start.1 = (f32[368,128]{1,0:T(8,128)}, f32[368,128]{1,0:T(8,128)S(1)}, u32[]{:S(2)}, u32[]{:S(2)}) collective-permute-start(f32[368,128]{1,0:T(8,128)} %get-tuple-element.10), channel_id=1, source_target_pairs={{4,0},{8,4},{12,8},{16,12},{20,16},{24,20},{28,24},{32,28},{36,32}... | collective-permute-start | bytes 565256 | tf_op jit(solution)/shard_map/ppermute | solution.py:252
  15.0 26.6 %all-to-all-start = ((f32[128,1,128]{2,1,0:T(1,128)}), f32[128,1,128]{2,1,0:T(1,128)S(1)}, u32[]{:S(2)}, u32[]{:S(2)}) async-start(f32[128,1,128]{2,1,0:T(1,128)} %bitcast.23), calls=%async_computation | async-start | bytes 131072 | tf_op jit(solution)/shard_map/all_to_all | solution.py:238
  41.6 0.6 copy-start
  41.6 0.7 copy-start.2
  41.6 0.7 copy-start.3
  69.9 18.7 %all-to-all-start.2 = ((f32[128,1,128]{2,1,0:T(1,128)}), f32[128,1,128]{2,1,0:T(1,128)S(1)}, u32[]{:S(2)}, u32[]{:S(2)}) async-start(f32[128,1,128]{2,1,0:T(1,128)} %bitcast.24), calls=%async_computation.2 | async-start | bytes 131072 | tf_op jit(solution)/shard_map/all_to_all | solution.py:277
  88.6 0.6 copy-start.1

commit v2 on v1

--- a/solution.py
+++ b/solution.py
@@ -6,6 +6,7 @@
 from jax.experimental.pallas import tpu as pltpu
 from jax.sharding import PartitionSpec as P
 
+
 BLK = "blk"
 DIR = "dir"
 VMEM = pltpu.VMEM
@@ -19,6 +20,8 @@
 RATIO_STEP = 1.1
 
 LANES = 128
+MIB = 1 << 20
+UNROLL = 18
 ROWS = 16
 CUR_X, CUR_Y, WIND_X, WIND_Y, ICE = 0, 24, 48, 64, 80
 
@@ -73,14 +76,17 @@
     low_ref,
     high_ref,
     slot_ref,
-    moved_ref,
+    stored_ref,
     parts_ref,
     cell_ref,
     turned_ref,
     sx_ref,
     sy_ref,
+    sw_ref,
     s16_ref,
     f16_ref,
+    moved_ref,
+    sems,
 ):
     shape = (ROWS, LANES)
     row, lane = lax.broadcasted_iota(jnp.int32, shape, 0), lane_of(shape)
@@ -104,6 +110,7 @@
     flow_16 = open_16 * (turned_ref[CUR_X + ROWS : CUR_X + ROWS + 1, :] + turned_ref[CUR_X + ROWS + 1 : CUR_X + ROWS + 2, :])
     cur_y = turned_ref[CUR_Y : CUR_Y + ROWS, :]
     flow_y = open_y * (cur_y + next_y(cur_y))
+    flow_w = pltpu.roll(flow_y, 1, 1)
 
     owner, place = jnp.maximum(slots, 0) // 16, jnp.where(slots >= 0, slots % 16, -1)
     wind_x, wind_y, ice = (jnp.zeros(shape, jnp.float32) for _ in range(3))
@@ -124,15 +131,18 @@
         base = pl.multiple_of(k * ROWS, ROWS)
         speed = speed_ref[pl.ds(base, ROWS), :]
         sx_ref[pl.ds(base, ROWS), :] = open_x * (speed + shifted_down(speed, low_ref[pl.ds(bins + k, 1), :]))
-        sy_ref[pl.ds(base, ROWS), :] = open_y * (speed + next_y(speed))
+        side = open_y * (speed + next_y(speed))
+        sy_ref[pl.ds(base, ROWS), :] = side
+        sw_ref[pl.ds(base, ROWS), :] = pltpu.roll(side, 1, 1)
         return 0
 
-    lax.fori_loop(0, freqs, faces, 0, unroll=4)
+    lax.fori_loop(0, freqs, faces, 0, unroll=12)
     s16_ref[...] = open_16 * (speed_ref[pl.ds(ROWS - 1, freqs, stride=ROWS), :] + high_ref[bins : bins + freqs, :])
 
     zero = jnp.zeros(shape, jnp.float32)
     moment, stress_x, stress_y, drift_x, drift_y, damp_x, damp_y = (zero,) * 7
     at = at_ref[0]
+    copies = []
     for j in range(dirs):
         cosine, sine = trig_ref[at, j], trig_ref[at, dirs + j]
         face = s16_ref[...] * cosine + flow_16
@@ -154,7 +164,8 @@
             )
             v = sy_ref[pl.ds(base, ROWS), :] * sine + flow_y
             right = v * jnp.where(v > 0.0, energy, next_y(energy))
-            left = pltpu.roll(right, 1, 1)
+            w = sw_ref[pl.ds(base, ROWS), :] * sine + flow_w
+            left = w * jnp.where(w > 0.0, pltpu.roll(energy, 1, 1), energy)
             moved = sea * (energy - ((above - below) + (right - left)))
             moved_ref[pl.ds(here, ROWS), :] = moved
             return (
@@ -163,7 +174,13 @@
                 fourth * (RATIO_STEP**-4) + moved,
             )
 
-        second, third, fourth = lax.fori_loop(0, freqs, step, (zero, zero, zero), unroll=4)
+        def out_copy():
+            part = pl.ds(j * freqs * ROWS, freqs * ROWS)
+            return pltpu.make_async_copy(moved_ref.at[part, :], stored_ref.at[part, :], sems.at[j])
+
+        second, third, fourth = lax.fori_loop(0, freqs, step, (zero, zero, zero), unroll=UNROLL)
+        copies.append(out_copy())
+        copies[-1].start()
         wind_gain = gain * jnp.maximum(wind_x * cosine + wind_y * sine, 0.0)
         push = wind_gain * second
         drift = third + wind_gain * fourth
@@ -178,6 +195,8 @@
         parts_ref[c, 0:16, :] = moment
         parts_ref[c, 16:32, :] = main
         parts_ref[c, 32:48, :] = damped
+    for copy in copies:
+        copy.wait()
 
 
 def forcing_kernel(at_ref, parts_ref, damping_ref, out_ref):
@@ -195,10 +214,9 @@
     cosine, sine = trig_ref[at, j], trig_ref[at, dirs + j]
     wind = jnp.maximum(cell_ref[0:16, :] * cosine + cell_ref[16:32, :] * sine, 0.0)
     growth = cell_ref[32:48, :] * wind - damping_ref[...]
-    start = pl.multiple_of(j * freqs * ROWS, ROWS)
     for k in range(freqs):
         ratio = RATIO_STEP ** (k - freqs + 1)
-        out_ref[k * ROWS : (k + 1) * ROWS, :] = moved_ref[pl.ds(start + k * ROWS, ROWS), :] * (1.0 + ratio * growth)
+        out_ref[k * ROWS : (k + 1) * ROWS, :] = moved_ref[k * ROWS : (k + 1) * ROWS, :] * (1.0 + ratio * growth)
 
 
 def row_kernel(got_ref, out_ref):
@@ -213,7 +231,15 @@
     return jax.ShapeDtypeStruct(shape, jnp.float32)
 
 
-def on_device(spectrum, group_speed, ocean_current, route_slot, wind_vector, ice_cover):
+def near(*shape):
+    return VMEM(shape, jnp.float32)
+
+
+def held(value):
+    return pltpu.with_memory_space_constraint(value, VMEM)
+
+
+def one_step(spectrum, group_speed, ocean_current, route_slot, wind_vector, ice_cover):
     dirs, freqs, _, _ = spectrum.shape
     bands, blocks = lax.axis_size(DIR), lax.axis_size(BLK)
     bins = dirs * freqs
@@ -225,78 +251,88 @@
 
     messages = pl.pallas_call(
         message_kernel,
-        out_shape=f32(LANES, LANES),
+        out_shape=near(LANES, LANES),
         in_specs=vmem_specs(3),
         out_specs=vmem_specs(1)[0],
         scratch_shapes=[VMEM((2, ROWS, LANES), jnp.float32)],
         name="messages",
+        compiler_params=pltpu.CompilerParams(vmem_limit_bytes=4 * MIB),
     )(
         ocean_current.reshape(2, ROWS, LANES),
         wind_vector.reshape(2, ROWS * LANES),
         ice_cover.reshape(ROWS, LANES),
     )
-    got = lax.all_to_all(messages, BLK, 0, 0, tiled=True)
-
-    flat = spectrum.reshape(bins * ROWS, LANES)
-    speed = group_speed.reshape(freqs * ROWS, LANES)
-    edge = f32(bins + freqs + 8, LANES)
-    last, first = pl.pallas_call(
+    got = held(lax.all_to_all(messages, BLK, 0, 0, tiled=True))
+
+    flat = held(spectrum.reshape(bins * ROWS, LANES))
+    speed = held(group_speed.reshape(freqs * ROWS, LANES))
+    edge = near(bins + freqs + 8, LANES)
+    edges = pl.pallas_call(
         lambda *refs: edge_kernel(bins, freqs, *refs),
         out_shape=(edge, edge),
         in_specs=vmem_specs(3),
         out_specs=tuple(vmem_specs(2)),
         name="edges",
-    )(flat, speed, route_slot)
+        compiler_params=pltpu.CompilerParams(vmem_limit_bytes=4 * MIB),
+    )
+    last, first = edges(flat, speed, route_slot)
     up = [(i, i + 1) for i in range(blocks - 1)]
-    low = lax.ppermute(last, BLK, up)
-    high = lax.ppermute(first, BLK, [(j, i) for i, j in up])
+    low = held(lax.ppermute(last, BLK, up))
+    high = held(lax.ppermute(first, BLK, [(j, i) for i, j in up]))
 
     moved, parts, cell = pl.pallas_call(
         lambda *refs: move_kernel(dirs, freqs, *refs),
-        out_shape=(f32(bins * ROWS, LANES), f32(bands, 48, LANES), f32(48, LANES)),
+        out_shape=(pltpu.HBM((bins * ROWS, LANES), jnp.float32), near(bands, 48, LANES), near(48, LANES)),
         in_specs=[smem, smem] + vmem_specs(6),
-        out_specs=tuple(vmem_specs(3)),
+        out_specs=(pl.BlockSpec(memory_space=pltpu.HBM), *vmem_specs(2)),
         scratch_shapes=[
             VMEM((LANES, LANES), jnp.float32),
             VMEM((freqs * ROWS, LANES), jnp.float32),
             VMEM((freqs * ROWS, LANES), jnp.float32),
+            VMEM((freqs * ROWS, LANES), jnp.float32),
             VMEM((freqs, LANES), jnp.float32),
             VMEM((freqs, LANES), jnp.float32),
+            VMEM((bins * ROWS, LANES), jnp.float32),
+            pltpu.SemaphoreType.DMA((dirs,)),
         ],
         name="move",
+        compiler_params=pltpu.CompilerParams(vmem_limit_bytes=8 * MIB),
     )(at, trig, got, flat, speed, low, high, route_slot)
 
-    parts = lax.all_to_all(parts, DIR, 0, 0, tiled=True)
+    parts = held(lax.all_to_all(parts, DIR, 0, 0, tiled=True))
     damping, own = pl.pallas_call(
         forcing_kernel,
-        out_shape=(f32(ROWS, LANES), f32(LANES, LANES)),
+        out_shape=(near(ROWS, LANES), near(LANES, LANES)),
         in_specs=[smem] + vmem_specs(1),
         out_specs=tuple(vmem_specs(2)),
         name="forcing",
+        compiler_params=pltpu.CompilerParams(vmem_limit_bytes=4 * MIB),
     )(at, parts)
-    ocean = lax.all_to_all(own, BLK, 0, 0, tiled=True)
+    ocean = held(lax.all_to_all(own, BLK, 0, 0, tiled=True))
     result = pl.pallas_call(
         lambda *refs: update_kernel(dirs, freqs, *refs),
         out_shape=f32(bins * ROWS, LANES),
         grid=(dirs,),
-        in_specs=[smem, smem] + vmem_specs(3),
+        in_specs=[smem, smem, pl.BlockSpec((freqs * ROWS, LANES), lambda j: (j, 0))] + vmem_specs(2),
         out_specs=pl.BlockSpec((freqs * ROWS, LANES), lambda j: (j, 0)),
         name="update",
+        compiler_params=pltpu.CompilerParams(vmem_limit_bytes=4 * MIB),
         cost_estimate=pl.CostEstimate(flops=3 * bins * ROWS * LANES, bytes_accessed=8 * bins * ROWS * LANES, transcendentals=0),
-    )(at, trig, moved, cell, damping)
+    )(at, trig, pltpu.with_memory_space_constraint(moved, pltpu.HBM), cell, damping)
     ocean = pl.pallas_call(
         row_kernel,
         out_shape=f32(ROWS, LANES),
         in_specs=vmem_specs(1),
         out_specs=vmem_specs(1)[0],
         name="rows",
+        compiler_params=pltpu.CompilerParams(vmem_limit_bytes=4 * MIB),
     )(ocean)
     return (result.reshape(spectrum.shape), ocean.reshape(1, 1, ROWS * LANES))
 
 
 def solution(mesh):
     return jax.shard_map(
-        on_device,
+        one_step,
         mesh=mesh,
         in_specs=(
             P(DIR, None, BLK, None),

time: 91.3 us -> 78.8 us (0.86)
  Pallas kernels: 30.2 us -> 15.1 us
  local copies, waits for them, and re-layouts: 1.37 us -> 4.86 us
    pallas_call x6, Pallas kernels: 30.2 us -> 15.1 us  [the longest x1 6.5 us: one_step(): pl.pallas_call(lambda *refs: update_kernel(dirs, freqs, *refs), out_shape...]
    unnamed x8 -> x20, local copies, waits for them, and re-layouts: 1.37 us -> 4.86 us
  transfers between devices with their start and end apart: 4 -> 4, of which waited for: 2 -> 2; matrix products, arithmetic and copies ran while one was open for 0% -> 0% of each run, Pallas kernels for 8% -> 9%
where the time goes in v2:
time: 78.8 us; the launch traced here: 78.2 us
  starting transfers between devices  32.4 us (41%)
  waiting for transfers between devices  16.6 us (21%)
  Pallas kernels  15.1 us (19%)
  blocking collectives  8.47 us (11%)
  local copies, waits for them, and re-layouts  4.86 us (6%)
    all_to_all x1, starting transfers between devices, one_step(): got = held(lax.all_to_all(messages, BLK, 0, 0, tiled=True))  15.1 us
    all_to_all x1, waiting for transfers between devices, one_step(): got = held(lax.all_to_all(messages, BLK, 0, 0, tiled=True))  11.5 us
    all_to_all x1, blocking collectives, one_step(): parts = held(lax.all_to_all(parts, DIR, 0, 0, tiled=True))  8.47 us
    all_to_all x1, starting transfers between devices, one_step(): ocean = held(lax.all_to_all(own, BLK, 0, 0, tiled=True))  7.11 us
    pallas_call x1, Pallas kernels, one_step(): pl.pallas_call(lambda *refs: update_kernel(dirs, freqs, *refs), out_shape...  6.5 us
    ppermute x1, starting transfers between devices, one_step(): high = held(lax.ppermute(first, BLK, [(j, i) for i, j in up]))  5.46 us
    pallas_call x1, Pallas kernels, one_step(): pl.pallas_call(lambda *refs: move_kernel(dirs, freqs, *refs), out_shape=(...  5.4 us
    all_to_all x1, waiting for transfers between devices, one_step(): ocean = held(lax.all_to_all(own, BLK, 0, 0, tiled=True))  5.11 us
  transfers between devices with their start and end apart: 4, of which 2 were waited for; matrix products, arithmetic and copies ran while one was open for 0% of the time, Pallas kernels for 9%

profile of v2, /device:TPU:1, one launch (start us, length us, event | category | flops | bytes accessed | tf_op | source)
XLA Modules:
  0.0 78.2 jit_solution(2082576756578078375)
XLA Ops:
  0.6 0.0 copy-start.8
  0.7 1.7 %copy-done = f32[9,36,16,128]{3,2,1,0:T(8,128)S(1)} copy-done((f32[9,36,16,128]{3,2,1,0:T(8,128)S(1)}, f32[9,36,16,128]{3,2,1,0:T(8,128)}, u32[]{:S(2)}) %copy-start) | copy-done | bytes 2654232
  2.4 1.0 %copy-done.2 = f32[36,16,128]{2,1,0:T(8,128)S(1)} copy-done((f32[36,16,128]{2,1,0:T(8,128)S(1)}, f32[36,16,128]{2,1,0:T(8,128)}, u32[]{:S(2)}) %copy-start.2) | copy-done | bytes 294936
  3.4 0.7 copy-done.4
  4.1 0.9 %edges.1 = (f32[368,128]{1,0:T(8,128)}, f32[368,128]{1,0:T(8,128)}) custom-call(f32[5184,128]{1,0:T(8,128)S(1)} %bitcast.16, f32[576,128]{1,0:T(8,128)S(1)} %bitcast.18, s32[16,128]{1,0:T(8,128)S(1)} %copy-done.4), custom_call_target="tpu_custom_call" | custom-call | tf_op jit(solution)/shard_map/edges/pallas_call | solution.py:278
  5.0 4.7 %collective-permute-start = (f32[368,128]{1,0:T(8,128)}, f32[368,128]{1,0:T(8,128)S(1)}, u32[]{:S(2)}, u32[]{:S(2)}) collective-permute-start(f32[368,128]{1,0:T(8,128)} %get-tuple-element.9), channel_id=1, source_target_pairs={{0,4},{4,8},{8,12},{12,16},{16,20},{20,24},{24,28},{28,32},{32,36}... | collective-permute-start | bytes 565256 | tf_op jit(solution)/shard_map/ppermute | solution.py:280
  9.7 5.5 %collective-permute-start.1 = (f32[368,128]{1,0:T(8,128)}, f32[368,128]{1,0:T(8,128)S(1)}, u32[]{:S(2)}, u32[]{:S(2)}) collective-permute-start(f32[368,128]{1,0:T(8,128)} %get-tuple-element.10), channel_id=1, source_target_pairs={{4,0},{8,4},{12,8},{16,12},{20,16},{24,20},{28,24},{32,28},{36,32}... | collective-permute-start | bytes 565256 | tf_op jit(solution)/shard_map/ppermute | solution.py:281
  15.2 0.0 copy-done.9
  15.2 0.0 copy-start.6
  15.2 0.7 copy-done.6
  15.9 0.7 copy-done.7
  16.6 0.9 %messages.1 = f32[128,128]{1,0:T(8,128)} custom-call(f32[2,16,128]{2,1,0:T(8,128)S(1)} %bitcast.22, f32[2,2048]{1,0:T(2,128)S(1)} %bitcast.23, f32[16,128]{1,0:T(8,128)S(1)} %bitcast.24), custom_call_target="tpu_custom_call" | custom-call | tf_op jit(solution)/shard_map/messages/pallas_call | solution.py:252
  17.5 15.1 %all-to-all-start = ((f32[128,1,128]{2,1,0:T(1,128)}), f32[128,1,128]{2,1,0:T(1,128)S(1)}, u32[]{:S(2)}, u32[]{:S(2)}) async-start(f32[128,1,128]{2,1,0:T(1,128)} %bitcast.5), calls=%async_computation | async-start | bytes 131072 | tf_op jit(solution)/shard_map/all_to_all | solution.py:265
  32.7 11.5 %all-to-all-done = f32[128,1,128]{2,1,0:T(1,128)S(1)} async-done(((f32[128,1,128]{2,1,0:T(1,128)}), f32[128,1,128]{2,1,0:T(1,128)S(1)}, u32[]{:S(2)}, u32[]{:S(2)}) %all-to-all-start) | async-done | bytes 65568 | tf_op jit(solution)/shard_map/all_to_all | solution.py:265
  44.1 0.0 collective-permute-done.refs_5_
  44.1 0.0 collective-permute-done.1.refs_6_
  44.1 0.0 copy-done.8
  44.2 5.4 %move.1 = (f32[5184,128]{1,0:T(8,128)}, f32[4,48,128]{2,1,0:T(8,128)S(1)}, f32[48,128]{1,0:T(8,128)S(1)}) custom-call(s32[1]{0:T(128)} %bitcast.refs_0_.at_ref, f32[4,18]{1,0:T(4,128)S(1)} %copy-done.8, f32[128,128]{1,0:T(8,128)S(1)} %bitcast.20, f32[5184,128]{1,0:T(8,128)S(1)} %bitcast.17, f32[576,128]{1,0:T(8,128)S(1)} %bitcast.19, ...), custom_call_target="tpu_custom_call" | custom-call | tf_op jit(solution)/shard_map/move/pallas_call | solution.py:283
  49.6 8.5 %all_to_all.27.parts_ref = f32[4,48,128]{2,1,0:T(8,128)S(1)} all-to-all(f32[4,48,128]{2,1,0:T(8,128)S(1)} %get-tuple-element.13), channel_id=1, replica_groups=mesh['blk'=128,'dir'=4] {'dir'}, dimensions={0} | all-to-all | bytes 196608 | tf_op jit(solution)/shard_map/all_to_all | solution.py:302
  58.1 0.7 forcing.1
  58.8 7.1 %all-to-all-start.2 = ((f32[128,1,128]{2,1,0:T(1,128)}), f32[128,1,128]{2,1,0:T(1,128)S(1)}, u32[]{:S(2)}, u32[]{:S(2)}) async-start(f32[128,1,128]{2,1,0:T(1,128)} %bitcast.11), calls=%async_computation.2 | async-start | bytes 131072 | tf_op jit(solution)/shard_map/all_to_all | solution.py:311
  65.9 6.5 %update.1 = f32[5184,128]{1,0:T(8,128)} custom-call(s32[1]{0:T(128)} %bitcast.refs_0_.at_ref, f32[4,18]{1,0:T(4,128)S(1)} %copy-done.8, f32[5184,128]{1,0:T(8,128)} %get-tuple-element.11.refs_2_, f32[48,128]{1,0:T(8,128)S(1)} %get-tuple-element.12.refs_3_, f32[16,128]{1,0:T(8,128)S(1)} %get-tuple-element.14.refs_4_), custom_call_target="tpu_custom_call" | custom-call | flops 1990656 | bytes 5308416 | tf_op jit(solution)/shard_map/update/pallas_call | solution.py:312
  72.4 5.1 %all-to-all-done.2 = f32[128,1,128]{2,1,0:T(1,128)S(1)} async-done(((f32[128,1,128]{2,1,0:T(1,128)}), f32[128,1,128]{2,1,0:T(1,128)S(1)}, u32[]{:S(2)}, u32[]{:S(2)}) %all-to-all-start.2) | async-done | bytes 65568 | tf_op jit(solution)/shard_map/all_to_all | solution.py:311
  77.5 0.7 rows.1
  (11 shorter events, 0.0 us)
Async XLA Ops:
  0.6 43.5 %copy-start.8 = (f32[4,18]{1,0:T(4,128)S(1)}, f32[4,18]{1,0:T(4,128)}, u32[]{:S(2)}) copy-start(f32[4,18]{1,0:T(4,128)} %constant.6.clone.refs_1_) | copy-start | bytes 868
  0.6 1.8 %copy-start = (f32[9,36,16,128]{3,2,1,0:T(8,128)S(1)}, f32[9,36,16,128]{3,2,1,0:T(8,128)}, u32[]{:S(2)}) copy-start(f32[9,36,16,128]{3,2,1,0:T(8,128)} %param.7) | copy-start | bytes 7962628
  2.4 1.0 %copy-start.2 = (f32[36,16,128]{2,1,0:T(8,128)S(1)}, f32[36,16,128]{2,1,0:T(8,128)}, u32[]{:S(2)}) copy-start(f32[36,16,128]{2,1,0:T(8,128)} %param.8) | copy-start | bytes 884740
  3.4 0.7 copy-start.4
  4.1 11.1 %copy-start.9 = (f32[1,2048]{1,0:T(1,128)S(1)}, f32[1,2048]{1,0:T(1,128)}, u32[]{:S(2)}) copy-start(f32[1,2048]{1,0:T(1,128)} %param.12) | copy-start | bytes 24580
  4.1 40.1 %copy-start.1 = (f32[9,36,16,128]{3,2,1,0:T(8,128)S(1)}, f32[9,36,16,128]{3,2,1,0:T(8,128)}, u32[]{:S(2)}) copy-start(f32[9,36,16,128]{3,2,1,0:T(8,128)} %param.7) | copy-start | bytes 7962628
  4.1 40.1 %copy-start.3 = (f32[36,16,128]{2,1,0:T(8,128)S(1)}, f32[36,16,128]{2,1,0:T(8,128)}, u32[]{:S(2)}) copy-start(f32[36,16,128]{2,1,0:T(8,128)} %param.8) | copy-start | bytes 884740
  4.1 40.1 %copy-start.5 = (s32[16,128]{1,0:T(8,128)S(1)}, s32[16,128]{1,0:T(8,128)}, u32[]{:S(2)}) copy-start(s32[16,128]{1,0:T(8,128)} %refs_7_.1) | copy-start | bytes 24580
  5.0 39.1 %collective-permute-start = (f32[368,128]{1,0:T(8,128)}, f32[368,128]{1,0:T(8,128)S(1)}, u32[]{:S(2)}, u32[]{:S(2)}) collective-permute-start(f32[368,128]{1,0:T(8,128)} %get-tuple-element.9), channel_id=1, source_target_pairs={{0,4},{4,8},{8,12},{12,16},{16,20},{20,24},{24,28},{28,32},{32,36}... | collective-permute-start | bytes 565256 | tf_op jit(solution)/shard_map/ppermute | solution.py:280
  9.7 34.4 %collective-permute-start.1 = (f32[368,128]{1,0:T(8,128)}, f32[368,128]{1,0:T(8,128)S(1)}, u32[]{:S(2)}, u32[]{:S(2)}) collective-permute-start(f32[368,128]{1,0:T(8,128)} %get-tuple-element.10), channel_id=1, source_target_pairs={{4,0},{8,4},{12,8},{16,12},{20,16},{24,20},{28,24},{32,28},{36,32}... | collective-permute-start | bytes 565256 | tf_op jit(solution)/shard_map/ppermute | solution.py:281
  15.2 0.7 copy-start.6
  15.9 0.7 copy-start.7
  17.5 26.6 %all-to-all-start = ((f32[128,1,128]{2,1,0:T(1,128)}), f32[128,1,128]{2,1,0:T(1,128)S(1)}, u32[]{:S(2)}, u32[]{:S(2)}) async-start(f32[128,1,128]{2,1,0:T(1,128)} %bitcast.5), calls=%async_computation | async-start | bytes 131072 | tf_op jit(solution)/shard_map/all_to_all | solution.py:265
  58.8 18.7 %all-to-all-start.2 = ((f32[128,1,128]{2,1,0:T(1,128)}), f32[128,1,128]{2,1,0:T(1,128)S(1)}, u32[]{:S(2)}, u32[]{:S(2)}) async-start(f32[128,1,128]{2,1,0:T(1,128)} %bitcast.11), calls=%async_computation.2 | async-start | bytes 131072 | tf_op jit(solution)/shard_map/all_to_all | solution.py:311
